TPU v7x, 256 devices: a whole 4x4x8 slice. The times are simulated.
256 devices in a mesh: dp: 4 (over x_hi, core), ctx: 64 (over z, y, x_lo).
Axes of the slice: x: 4 (x_hi: 2, x_lo: 2; x = x_hi * 2 + x_lo), y: 4, z: 8, core: 2. Of those that a mesh axis runs over, the one named last changes fastest.
Arguments:
- queries: bfloat16 [4, 8192, 2560], P('dp', 'ctx'), may hold values from -6 to 6
- keys: bfloat16 [4, 8192, 512], P('dp', 'ctx'), may hold values from -6 to 6
- values: bfloat16 [4, 8192, 512], P('dp', 'ctx'), may hold values from -6 to 6
- out_grad: bfloat16 [4, 8192, 2560], P('dp', 'ctx'), may hold values from -24 to 24
- layer_input: bfloat16 [4, 8192, 5120], P('dp', 'ctx'), may hold values from -16 to 16
- doc_lens: int32 [4, 16], P('dp'), may hold values from 1 to 1024, 8192 in all within a row
Outputs:
- attn_out: bfloat16 [4, 8192, 2560], P('dp', 'ctx')
- query_grad: bfloat16 [4, 8192, 2560], P('dp', 'ctx')
- key_grad: bfloat16 [4, 8192, 512], P('dp', 'ctx')
- value_grad: bfloat16 [4, 8192, 512], P('dp', 'ctx')
- weight_grad: float32 [5120, 1024], P(('dp', 'ctx'))
Inputs may be any that keep to these rules, and one draw needn't show every extreme that they name: `doc_lens`: the documents of a micro-batch lie end to end and fill its 8192 positions; in every micro-batch the longest has exactly 1024 positions.
All inputs are finite; a program needn't handle non-finite values.
Results may differ from a plain program's by a relative error of at most 0.029.
Values may be sent and summed in bfloat16 or wider, within the bound.
No kernel may reach another device: no remote copies, remote signals or barrier semaphores. Data moves between devices by JAX's collectives and lax.ppermute only.
A program may use at most 128 MiB of HBM per device.

v0:
```python
import math

import jax
import jax.numpy as jnp
from jax import lax
from jax.sharding import PartitionSpec as P

D = 5120
HD = 128


NEGATIVE = -1e30


def from_behind(block, axis, distance):
    devices = range(lax.axis_size(axis))
    route = [(i - distance, i) for i in devices if i - distance in devices]
    return lax.ppermute(block, axis, route)


def doc_index(lengths_row, positions):
    bounds = jnp.cumsum(lengths_row)
    return jnp.sum((positions[:, None] >= bounds[None, :]).astype(jnp.int32), axis=1)


def shards(queries, keys, values, out_grad, layer_input, doc_lens):
    tok_rows = queries.shape[1]
    kv_width = keys.shape[2]
    heads_kv = kv_width // HD
    group = queries.shape[2] // kv_width
    inverse = 1.0 / math.sqrt(HD)
    blocks_back = min(8, lax.axis_size("ctx") // 4)
    own_pair = jnp.concatenate([keys[0], values[0]], axis=1)
    earlier = []
    moving = own_pair
    for distance in range(blocks_back):
        moving = from_behind(moving, "ctx", 1)
        earlier.append(moving)
    window_pair = jnp.concatenate(earlier[::-1] + [own_pair], axis=0)
    span = window_pair.shape[0]
    key_win = window_pair[:, :kv_width].reshape(span, heads_kv, HD)
    value_win = window_pair[:, kv_width:].reshape(span, heads_kv, HD)
    device = lax.axis_index("ctx")
    query_pos = device * tok_rows + jnp.arange(tok_rows, dtype=jnp.int32)
    key_pos = (device - blocks_back) * tok_rows + jnp.arange(span, dtype=jnp.int32)
    query_ids = doc_index(doc_lens[0], query_pos)
    key_ids = doc_index(doc_lens[0], key_pos)
    allowed = (
        (key_pos[None, :] <= query_pos[:, None])
        & (key_ids[None, :] == query_ids[:, None])
        & (key_pos[None, :] >= 0)
    )
    query_blk = queries[0].reshape(tok_rows, heads_kv, group, HD)
    grad_blk = out_grad[0].reshape(tok_rows, heads_kv, group, HD)
    scores = (
        jnp.einsum("ighd,jgd->ghij", query_blk, key_win, preferred_element_type=jnp.float32)
        * inverse
    )
    scores = jnp.where(allowed[None, None], scores, NEGATIVE)
    peak = jnp.max(scores, axis=-1, keepdims=True)
    exponent = jnp.exp(scores - peak)
    probs = exponent / jnp.sum(exponent, axis=-1, keepdims=True)
    probs_half = probs.astype(jnp.bfloat16)
    output = jnp.einsum("ghij,jgd->ighd", probs_half, value_win, preferred_element_type=jnp.float32)
    out_half = output.astype(jnp.bfloat16)
    delta = jnp.einsum("ighd,ighd->ghi", grad_blk, out_half, preferred_element_type=jnp.float32)
    prob_grad = jnp.einsum(
        "ighd,jgd->ghij", grad_blk, value_win, preferred_element_type=jnp.float32
    )
    score_grad = (probs * (prob_grad - delta[..., None])).astype(jnp.bfloat16)
    query_part = (
        jnp.einsum("ghij,jgd->ighd", score_grad, key_win, preferred_element_type=jnp.float32)
        * inverse
    ).astype(jnp.bfloat16)
    key_part = (
        jnp.einsum("ghij,ighd->jgd", score_grad, query_blk, preferred_element_type=jnp.float32)
        * inverse
    )
    value_part = jnp.einsum(
        "ghij,ighd->jgd", probs_half, grad_blk, preferred_element_type=jnp.float32
    )
    pair_grad = jnp.concatenate(
        [key_part.reshape(span, kv_width), value_part.reshape(span, kv_width)], axis=1
    )

    def block_back(distance):
        first_row = (blocks_back - distance) * tok_rows
        return pair_grad[first_row : first_row + tok_rows]

    gathered_back = block_back(blocks_back)
    for distance in range(blocks_back, 0, -1):
        gathered_back = from_behind(gathered_back, "ctx", -1) + block_back(distance - 1)
    pair_half = gathered_back.astype(jnp.bfloat16)
    token_rows = layer_input[0]
    n_data = lax.axis_size("dp")
    n_context = lax.axis_size("ctx")
    grad_scale = 1.0 / math.sqrt(tok_rows * n_context * n_data)
    owned = D // (n_data * n_context)
    split_rows = token_rows.reshape(tok_rows, n_data, n_context * owned)
    column_share = lax.all_to_all(split_rows, "ctx", split_axis=2, concat_axis=0, tiled=True)
    column_share = column_share.reshape(tok_rows * n_context, n_data * owned)
    batch_grad = lax.dot_general(
        column_share,
        lax.all_gather(pair_half, "ctx", axis=0, tiled=True),
        (((0,), (0,)), ((), ())),
        preferred_element_type=jnp.float32,
    )
    weight_grad = lax.psum_scatter(batch_grad * grad_scale, "dp", scatter_dimension=0, tiled=True)
    attn_out = out_half.reshape(tok_rows, group * kv_width)[None]
    query_grad = query_part.reshape(tok_rows, group * kv_width)[None]
    key_grad = pair_half[:, :kv_width][None]
    value_grad = pair_half[:, kv_width:][None]
    return (attn_out, query_grad, key_grad, value_grad, weight_grad)


def solution(mesh):
    in_specs = (
        P("dp", "ctx", None),
        P("dp", "ctx", None),
        P("dp", "ctx", None),
        P("dp", "ctx", None),
        P("dp", "ctx", None),
        P("dp", None),
    )
    out_specs = (
        P("dp", "ctx", None),
        P("dp", "ctx", None),
        P("dp", "ctx", None),
        P("dp", "ctx", None),
        P(("dp", "ctx"), None),
    )
    return jax.shard_map(shards, mesh=mesh, in_specs=in_specs, out_specs=out_specs, check_vma=False)
```

profile of v0, /device:TPU:38, one launch (start us, length us, event | category | flops | bytes accessed | tf_op | source)
XLA Modules:
  0.0 713.2 jit_solution(14462757935560316021)
XLA Ops:
  13.1 6.2 collective-permute-done
  19.3 4.6 collective-permute-start.1
  23.9 6.5 collective-permute-done.1
  33.9 7.8 %collective-permute-done.2 = bf16[128,1024]{0,1:T(8,128)(2,1)S(1)} collective-permute-done((bf16[128,1024]{0,1:T(8,128)(2,1)S(1)}, bf16[128,1024]{0,1:T(8,128)(2,1)S(1)}, u32[]{:S(2)}, u32[]{:S(2)}) %collective-permute-start.2) | collective-permute-done | bytes 262176 | tf_op jit(solution)/shard_map/ppermute | solution.py:18
  43.6 9.1 %collective-permute-done.3 = bf16[128,1024]{0,1:T(8,128)(2,1)S(1)} collective-permute-done((bf16[128,1024]{0,1:T(8,128)(2,1)S(1)}, bf16[128,1024]{0,1:T(8,128)(2,1)S(1)}, u32[]{:S(2)}, u32[]{:S(2)}) %collective-permute-start.3) | collective-permute-done | bytes 262176 | tf_op jit(solution)/shard_map/ppermute | solution.py:18
  54.6 9.3 %collective-permute-done.4 = bf16[128,1024]{0,1:T(8,128)(2,1)S(1)} collective-permute-done((bf16[128,1024]{0,1:T(8,128)(2,1)S(1)}, bf16[128,1024]{0,1:T(8,128)(2,1)S(1)}, u32[]{:S(2)}, u32[]{:S(2)}) %collective-permute-start.4) | collective-permute-done | bytes 262176 | tf_op jit(solution)/shard_map/ppermute | solution.py:18
  65.9 9.4 %collective-permute-done.5 = bf16[128,1024]{0,1:T(8,128)(2,1)} collective-permute-done((bf16[128,1024]{0,1:T(8,128)(2,1)S(1)}, bf16[128,1024]{0,1:T(8,128)(2,1)}, u32[]{:S(2)}, u32[]{:S(2)}) %collective-permute-start.5) | collective-permute-done | bytes 262176 | tf_op jit(solution)/shard_map/ppermute | solution.py:18
  81.3 5.6 collective-permute-done.6
  91.5 6.9 collective-permute-done.7
  102.1 6.9 fusion.43
  109.0 5.9 fusion.8
  120.2 5.2 fusion.16
  125.4 5.6 fusion.3
  138.6 6.9 collective-permute-start.8
  145.5 12.1 %collective-permute-done.8 = f32[128,1024]{1,0:T(8,128)S(1)} collective-permute-done((f32[128,1024]{1,0:T(8,128)S(1)}, f32[128,1024]{1,0:T(8,128)S(1)}, u32[]{:S(2)}, u32[]{:S(2)}) %collective-permute-start.8) | collective-permute-done | bytes 524320 | tf_op jit(solution)/shard_map/ppermute | solution.py:18
  162.0 12.6 %collective-permute-done.9 = f32[128,1024]{1,0:T(8,128)S(1)} collective-permute-done((f32[128,1024]{1,0:T(8,128)S(1)}, f32[128,1024]{1,0:T(8,128)S(1)}, u32[]{:S(2)}, u32[]{:S(2)}) %collective-permute-start.9) | collective-permute-done | bytes 524320 | tf_op jit(solution)/shard_map/ppermute | solution.py:18
  178.1 12.7 %collective-permute-done.10 = f32[128,1024]{1,0:T(8,128)S(1)} collective-permute-done((f32[128,1024]{1,0:T(8,128)S(1)}, f32[128,1024]{1,0:T(8,128)S(1)}, u32[]{:S(2)}, u32[]{:S(2)}) %collective-permute-start.10) | collective-permute-done | bytes 524320 | tf_op jit(solution)/shard_map/ppermute | solution.py:18
  193.0 13.1 %collective-permute-done.11 = f32[128,1024]{1,0:T(8,128)S(1)} collective-permute-done((f32[128,1024]{1,0:T(8,128)S(1)}, f32[128,1024]{1,0:T(8,128)S(1)}, u32[]{:S(2)}, u32[]{:S(2)}) %collective-permute-start.11) | collective-permute-done | bytes 524320 | tf_op jit(solution)/shard_map/ppermute | solution.py:18
  206.2 6.4 collective-permute-start.12
  212.6 11.2 %collective-permute-done.12 = f32[128,1024]{1,0:T(8,128)S(1)} collective-permute-done((f32[128,1024]{1,0:T(8,128)S(1)}, f32[128,1024]{1,0:T(8,128)S(1)}, u32[]{:S(2)}, u32[]{:S(2)}) %collective-permute-start.12) | collective-permute-done | bytes 524320 | tf_op jit(solution)/shard_map/ppermute | solution.py:18
  223.9 7.4 %collective-permute-start.13 = (f32[128,1024]{1,0:T(8,128)S(1)}, f32[128,1024]{1,0:T(8,128)S(1)}, u32[]{:S(2)}, u32[]{:S(2)}) collective-permute-start(f32[128,1024]{1,0:T(8,128)S(1)} %fusion.35), channel_id=1, source_target_pairs={{1,0},{2,1},{3,2},{4,3},{5,4},{6,5},{7,6},{8,7},{9,8},{10,9},{11,1... | collective-permute-start | bytes 1572872 | tf_op jit(solution)/shard_map/ppermute | solution.py:18
  231.3 10.4 %collective-permute-done.13 = f32[128,1024]{1,0:T(8,128)S(1)} collective-permute-done((f32[128,1024]{1,0:T(8,128)S(1)}, f32[128,1024]{1,0:T(8,128)S(1)}, u32[]{:S(2)}, u32[]{:S(2)}) %collective-permute-start.13) | collective-permute-done | bytes 524320 | tf_op jit(solution)/shard_map/ppermute | solution.py:18
  241.7 7.4 %collective-permute-start.14 = (f32[128,1024]{1,0:T(8,128)S(1)}, f32[128,1024]{1,0:T(8,128)S(1)}, u32[]{:S(2)}, u32[]{:S(2)}) collective-permute-start(f32[128,1024]{1,0:T(8,128)S(1)} %fusion.37), channel_id=1, source_target_pairs={{1,0},{2,1},{3,2},{4,3},{5,4},{6,5},{7,6},{8,7},{9,8},{10,9},{11,1... | collective-permute-start | bytes 1572872 | tf_op jit(solution)/shard_map/ppermute | solution.py:18
  249.1 9.5 %collective-permute-done.14 = f32[128,1024]{1,0:T(8,128)S(1)} collective-permute-done((f32[128,1024]{1,0:T(8,128)S(1)}, f32[128,1024]{1,0:T(8,128)S(1)}, u32[]{:S(2)}, u32[]{:S(2)}) %collective-permute-start.14) | collective-permute-done | bytes 524320 | tf_op jit(solution)/shard_map/ppermute | solution.py:18
  258.7 7.4 %collective-permute-start.15 = (f32[128,1024]{1,0:T(8,128)S(1)}, f32[128,1024]{1,0:T(8,128)S(1)}, u32[]{:S(2)}, u32[]{:S(2)}) collective-permute-start(f32[128,1024]{1,0:T(8,128)S(1)} %fusion.24), channel_id=1, source_target_pairs={{1,0},{2,1},{3,2},{4,3},{5,4},{6,5},{7,6},{8,7},{9,8},{10,9},{11,1... | collective-permute-start | bytes 1572872 | tf_op jit(solution)/shard_map/ppermute | solution.py:18
  266.1 6.7 collective-permute-done.15
  278.9 35.0 %all-to-all-start = ((bf16[128,4,1280]{0,1,2:T(4,128)(2,1)}), bf16[128,4,1280]{0,1,2:T(4,128)(2,1)S(1)}, u32[]{:S(2)}, u32[]{:S(2)}) async-start(bf16[128,4,1280]{0,1,2:T(4,128)(2,1)} %copy.80), calls=%async_computation | async-start | bytes 2621440 | tf_op jit(solution)/shard_map/all_to_all | solution.py:100
  315.2 4.8 fusion.12
  323.2 15.4 %all-to-all-done = bf16[128,4,1280]{0,1,2:T(4,128)(2,1)S(1)} async-done(((bf16[128,4,1280]{0,1,2:T(4,128)(2,1)}), bf16[128,4,1280]{0,1,2:T(4,128)(2,1)S(1)}, u32[]{:S(2)}, u32[]{:S(2)}) %all-to-all-start) | async-done | bytes 1310752 | tf_op jit(solution)/shard_map/all_to_all | solution.py:100
  339.0 337.5 %all-gather.2.cloned.1.call-done = bf16[8192,1024]{1,0:T(8,128)(2,1)} async-done(((bf16[128,1024]{1,0:T(8,128)(2,1)}), bf16[8192,1024]{1,0:T(8,128)(2,1)}) %all-gather.2.cloned.1.call-update) | async-done | bytes 16777232 | tf_op jit(solution)/shard_map/all_gather | solution.py:104
  676.4 9.1 %fusion.20 = f32[80,1024]{1,0:T(8,128)S(1)} fusion(bf16[8192,1024]{1,0:T(8,128)(2,1)} %all-gather.2.cloned.1.call-done, bf16[10,8,64,128]{3,2,1,0:T(8,128)(2,1)S(1)} %bitcast.98), kind=kOutput, calls=%fused_computation.40 | convolution fusion | flops 1342259200 | bytes 18415616 | tf_op jit(solution)/shard_map/dot_general | solution.py:102
  685.6 12.8 %fusion = f32[24,1024]{1,0:T(8,128)S(1)} fusion(f32[80,1024]{1,0:T(8,128)S(1)} %fusion.20), kind=kCustom, calls=%all-reduce-scatter | all-reduce-scatter fusion | flops 98305 | bytes 427008
  (87 shorter events, 70.5 us)
Async XLA Ops:
  7.2 72.9 %copy-start.10 = (bf16[1,128,2560]{2,1,0:T(8,128)(2,1)S(1)}, bf16[1,128,2560]{2,1,0:T(8,128)(2,1)}, u32[]{:S(2)}) copy-start(bf16[1,128,2560]{2,1,0:T(8,128)(2,1)} %param.6) | copy-start | bytes 1966084
  7.2 669.3 %all-gather.2.cloned.1.call-start = ((), (), s32[]{:S(2)}) async-start(), calls=%async_computation.1 | async-start | bytes 17039360 | tf_op jit(solution)/shard_map/all_gather | solution.py:104
  9.4 9.9 %collective-permute-start = (bf16[128,1024]{0,1:T(8,128)(2,1)S(1)}, bf16[128,1024]{0,1:T(8,128)(2,1)S(1)}, u32[]{:S(2)}, u32[]{:S(2)}) collective-permute-start(bf16[128,1024]{0,1:T(8,128)(2,1)S(1)} %pad_maximum_fusion.1), channel_id=1, source_target_pairs={{0,1},{1,2},{2,3},{3,4},{4,5},{5,6},{6,7},{7,8},{8,9},{9,10},{10,1... | collective-permute-start | bytes 786440 | tf_op jit(solution)/shard_map/ppermute | solution.py:18
  19.3 11.2 %collective-permute-start.1 = (bf16[128,1024]{0,1:T(8,128)(2,1)S(1)}, bf16[128,1024]{0,1:T(8,128)(2,1)S(1)}, u32[]{:S(2)}, u32[]{:S(2)}) collective-permute-start(bf16[128,1024]{0,1:T(8,128)(2,1)S(1)} %collective-permute-done), channel_id=1, source_target_pairs={{0,1},{1,2},{2,3},{3,4},{4,5},{5,6},{6,7},{7,8},{8,9},{9,10},{10,1... | collective-permute-start | bytes 786440 | tf_op jit(solution)/shard_map/ppermute | solution.py:18
  30.5 11.2 %collective-permute-start.2 = (bf16[128,1024]{0,1:T(8,128)(2,1)S(1)}, bf16[128,1024]{0,1:T(8,128)(2,1)S(1)}, u32[]{:S(2)}, u32[]{:S(2)}) collective-permute-start(bf16[128,1024]{0,1:T(8,128)(2,1)S(1)} %collective-permute-done.1), channel_id=1, source_target_pairs={{0,1},{1,2},{2,3},{3,4},{4,5},{5,6},{6,7},{7,8},{8,9},{9,10},{10,1... | collective-permute-start | bytes 786440 | tf_op jit(solution)/shard_map/ppermute | solution.py:18
  41.7 11.0 %collective-permute-start.3 = (bf16[128,1024]{0,1:T(8,128)(2,1)S(1)}, bf16[128,1024]{0,1:T(8,128)(2,1)S(1)}, u32[]{:S(2)}, u32[]{:S(2)}) collective-permute-start(bf16[128,1024]{0,1:T(8,128)(2,1)S(1)} %collective-permute-done.2), channel_id=1, source_target_pairs={{0,1},{1,2},{2,3},{3,4},{4,5},{5,6},{6,7},{7,8},{8,9},{9,10},{10,1... | collective-permute-start | bytes 786440 | tf_op jit(solution)/shard_map/ppermute | solution.py:18
  52.7 11.3 %collective-permute-start.4 = (bf16[128,1024]{0,1:T(8,128)(2,1)S(1)}, bf16[128,1024]{0,1:T(8,128)(2,1)S(1)}, u32[]{:S(2)}, u32[]{:S(2)}) collective-permute-start(bf16[128,1024]{0,1:T(8,128)(2,1)S(1)} %collective-permute-done.3), channel_id=1, source_target_pairs={{0,1},{1,2},{2,3},{3,4},{4,5},{5,6},{6,7},{7,8},{8,9},{9,10},{10,1... | collective-permute-start | bytes 786440 | tf_op jit(solution)/shard_map/ppermute | solution.py:18
  64.0 11.4 %collective-permute-start.5 = (bf16[128,1024]{0,1:T(8,128)(2,1)S(1)}, bf16[128,1024]{0,1:T(8,128)(2,1)}, u32[]{:S(2)}, u32[]{:S(2)}) collective-permute-start(bf16[128,1024]{0,1:T(8,128)(2,1)S(1)} %collective-permute-done.4), channel_id=1, source_target_pairs={{0,1},{1,2},{2,3},{3,4},{4,5},{5,6},{6,7},{7,8},{8,9},{9,10},{10,1... | collective-permute-start | bytes 786440 | tf_op jit(solution)/shard_map/ppermute | solution.py:18
  75.4 11.6 %collective-permute-start.6 = (bf16[128,1024]{0,1:T(8,128)(2,1)}, bf16[128,1024]{0,1:T(8,128)(2,1)}, u32[]{:S(2)}, u32[]{:S(2)}) collective-permute-start(bf16[128,1024]{0,1:T(8,128)(2,1)} %collective-permute-done.5), channel_id=1, source_target_pairs={{0,1},{1,2},{2,3},{3,4},{4,5},{5,6},{6,7},{7,8},{8,9},{9,10},{10,1... | collective-permute-start | bytes 786440 | tf_op jit(solution)/shard_map/ppermute | solution.py:18
  80.4 21.7 %copy-start.7 = (bf16[1,128,2560]{1,2,0:T(8,128)(2,1)}, bf16[1,128,2560]{1,2,0:T(8,128)(2,1)S(1)}, u32[]{:S(2)}) copy-start(bf16[1,128,2560]{1,2,0:T(8,128)(2,1)S(1)} %copy.68) | copy-start | bytes 1966084
  86.9 11.5 %collective-permute-start.7 = (bf16[128,1024]{0,1:T(8,128)(2,1)}, bf16[128,1024]{0,1:T(8,128)(2,1)S(1)}, u32[]{:S(2)}, u32[]{:S(2)}) collective-permute-start(bf16[128,1024]{0,1:T(8,128)(2,1)} %collective-permute-done.6), channel_id=1, source_target_pairs={{0,1},{1,2},{2,3},{3,4},{4,5},{5,6},{6,7},{7,8},{8,9},{9,10},{10,1... | collective-permute-start | bytes 786440 | tf_op jit(solution)/shard_map/ppermute | solution.py:18
  100.9 1.2 copy-start.11
  102.1 6.9 copy-start.4
  114.9 3.3 copy-start.1
  120.2 5.2 copy-start.3
  125.4 5.6 copy-start.8
  131.0 3.3 copy-start.2
  137.4 20.1 %copy-start = (f32[1152,512]{1,0:T(8,128)S(1)}, f32[1152,512]{1,0:T(8,128)}, u32[]{:S(2)}) copy-start(f32[1152,512]{1,0:T(8,128)} %copy.78) | copy-start | bytes 7077892
  138.6 19.0 %collective-permute-start.8 = (f32[128,1024]{1,0:T(8,128)S(1)}, f32[128,1024]{1,0:T(8,128)S(1)}, u32[]{:S(2)}, u32[]{:S(2)}) collective-permute-start(f32[128,1024]{1,0:T(8,128)S(1)} %fusion.25), channel_id=1, source_target_pairs={{1,0},{2,1},{3,2},{4,3},{5,4},{6,5},{7,6},{8,7},{9,8},{10,9},{11,1... | collective-permute-start | bytes 1572872 | tf_op jit(solution)/shard_map/ppermute | solution.py:18
  157.6 17.0 %collective-permute-start.9 = (f32[128,1024]{1,0:T(8,128)S(1)}, f32[128,1024]{1,0:T(8,128)S(1)}, u32[]{:S(2)}, u32[]{:S(2)}) collective-permute-start(f32[128,1024]{1,0:T(8,128)S(1)} %fusion.27), channel_id=1, source_target_pairs={{1,0},{2,1},{3,2},{4,3},{5,4},{6,5},{7,6},{8,7},{9,8},{10,9},{11,1... | collective-permute-start | bytes 1572872 | tf_op jit(solution)/shard_map/ppermute | solution.py:18
  174.7 16.1 %collective-permute-start.10 = (f32[128,1024]{1,0:T(8,128)S(1)}, f32[128,1024]{1,0:T(8,128)S(1)}, u32[]{:S(2)}, u32[]{:S(2)}) collective-permute-start(f32[128,1024]{1,0:T(8,128)S(1)} %fusion.29), channel_id=1, source_target_pairs={{1,0},{2,1},{3,2},{4,3},{5,4},{6,5},{7,6},{8,7},{9,8},{10,9},{11,1... | collective-permute-start | bytes 1572872 | tf_op jit(solution)/shard_map/ppermute | solution.py:18
  190.8 15.3 %collective-permute-start.11 = (f32[128,1024]{1,0:T(8,128)S(1)}, f32[128,1024]{1,0:T(8,128)S(1)}, u32[]{:S(2)}, u32[]{:S(2)}) collective-permute-start(f32[128,1024]{1,0:T(8,128)S(1)} %fusion.31), channel_id=1, source_target_pairs={{1,0},{2,1},{3,2},{4,3},{5,4},{6,5},{7,6},{8,7},{9,8},{10,9},{11,1... | collective-permute-start | bytes 1572872 | tf_op jit(solution)/shard_map/ppermute | solution.py:18
  206.2 17.7 %collective-permute-start.12 = (f32[128,1024]{1,0:T(8,128)S(1)}, f32[128,1024]{1,0:T(8,128)S(1)}, u32[]{:S(2)}, u32[]{:S(2)}) collective-permute-start(f32[128,1024]{1,0:T(8,128)S(1)} %fusion.33), channel_id=1, source_target_pairs={{1,0},{2,1},{3,2},{4,3},{5,4},{6,5},{7,6},{8,7},{9,8},{10,9},{11,1... | collective-permute-start | bytes 1572872 | tf_op jit(solution)/shard_map/ppermute | solution.py:18
  223.9 17.8 %collective-permute-start.13 = (f32[128,1024]{1,0:T(8,128)S(1)}, f32[128,1024]{1,0:T(8,128)S(1)}, u32[]{:S(2)}, u32[]{:S(2)}) collective-permute-start(f32[128,1024]{1,0:T(8,128)S(1)} %fusion.35), channel_id=1, source_target_pairs={{1,0},{2,1},{3,2},{4,3},{5,4},{6,5},{7,6},{8,7},{9,8},{10,9},{11,1... | collective-permute-start | bytes 1572872 | tf_op jit(solution)/shard_map/ppermute | solution.py:18
  241.7 16.9 %collective-permute-start.14 = (f32[128,1024]{1,0:T(8,128)S(1)}, f32[128,1024]{1,0:T(8,128)S(1)}, u32[]{:S(2)}, u32[]{:S(2)}) collective-permute-start(f32[128,1024]{1,0:T(8,128)S(1)} %fusion.37), channel_id=1, source_target_pairs={{1,0},{2,1},{3,2},{4,3},{5,4},{6,5},{7,6},{8,7},{9,8},{10,9},{11,1... | collective-permute-start | bytes 1572872 | tf_op jit(solution)/shard_map/ppermute | solution.py:18
  258.7 14.1 %collective-permute-start.15 = (f32[128,1024]{1,0:T(8,128)S(1)}, f32[128,1024]{1,0:T(8,128)S(1)}, u32[]{:S(2)}, u32[]{:S(2)}) collective-permute-start(f32[128,1024]{1,0:T(8,128)S(1)} %fusion.24), channel_id=1, source_target_pairs={{1,0},{2,1},{3,2},{4,3},{5,4},{6,5},{7,6},{8,7},{9,8},{10,9},{11,1... | collective-permute-start | bytes 1572872 | tf_op jit(solution)/shard_map/ppermute | solution.py:18
  276.5 37.4 %copy-start.12 = (u32[256]{0:T(256)S(1)}, u32[256]{0:T(256)}, u32[]{:S(2)}) copy-start(u32[256]{0:T(256)} %constant.37) | copy-start | bytes 3076
  278.9 36.2 %copy-start.5 = (bf16[1152,512]{0,1:T(8,128)(2,1)S(1)}, bf16[1152,512]{0,1:T(8,128)(2,1)}, u32[]{:S(2)}) copy-start(bf16[1152,512]{0,1:T(8,128)(2,1)} %copy-done.4) | copy-start | bytes 3538948
  278.9 59.7 %all-to-all-start = ((bf16[128,4,1280]{0,1,2:T(4,128)(2,1)}), bf16[128,4,1280]{0,1,2:T(4,128)(2,1)S(1)}, u32[]{:S(2)}, u32[]{:S(2)}) async-start(bf16[128,4,1280]{0,1,2:T(4,128)(2,1)} %copy.80), calls=%async_computation | async-start | bytes 2621440 | tf_op jit(solution)/shard_map/all_to_all | solution.py:100
  315.1 7.0 copy-start.6
  676.4 23.9 %copy-start.9 = (bf16[128,1024]{1,0:T(8,128)(2,1)S(1)}, bf16[128,1024]{1,0:T(8,128)(2,1)}, u32[]{:S(2)}) copy-start(bf16[128,1024]{1,0:T(8,128)(2,1)} %fusion.39) | copy-start | bytes 786436
  698.4 7.1 collective-permute-start.16
Sparse Core Ops, SparseCore 0:
  273.7 402.6 all-gather.1
where the time goes:
time: 714 us; the launch traced here: 713 us
  waiting for transfers between devices  507 us (71%)
  starting transfers between devices  104 us (15%)
  matrix products  38.2 us (5%)
  local copies, waits for them, and re-layouts  24.3 us (3%)
  between operations  15.2 us (2%)
  blocking collectives  12.8 us (2%)
  other arithmetic  12.4 us (2%)
    all_gather x1, waiting for transfers between devices, shards(): lax.all_gather(pair_half, 'ctx', axis=0, tiled=True)  337 us
    ppermute x16, waiting for transfers between devices, from_behind(): return lax.ppermute(block, axis, route)  149 us
    ppermute x16, starting transfers between devices, from_behind(): return lax.ppermute(block, axis, route)  66.9 us
    all_to_all x1, starting transfers between devices, shards(): lax.all_to_all(split_rows, 'ctx', split_axis=2, concat_axis=0, tiled=True)  35 us
    all_to_all x1, waiting for transfers between devices, shards(): lax.all_to_all(split_rows, 'ctx', split_axis=2, concat_axis=0, tiled=True)  15.4 us
  transfers between devices with their start and end apart: 19, of which 19 were waited for; matrix products, arithmetic and copies ran while one was open for 3% of the time, Pallas kernels for 0%

commit v1 on v0

v1 whole, which is shorter than its diff:
```python
import math

import jax
import jax.numpy as jnp
from jax import lax
from jax.sharding import Mesh
from jax.sharding import PartitionSpec as P

D = 5120
HD = 128


NEGATIVE = -1e30
CTX = ("cz", "cw")


def shifted(block, distance, n_ctx):
    route = [(i - distance, i) for i in range(n_ctx) if 0 <= i - distance < n_ctx]
    return lax.ppermute(block, CTX, route)


def doc_index(lengths_row, positions):
    bounds = jnp.cumsum(lengths_row)
    return jnp.sum((positions[:, None] >= bounds[None, :]).astype(jnp.int32), axis=1)


def make_shards(n_data, n_cz, n_cw):
    n_context = n_cz * n_cw

    def shards(queries, keys, values, out_grad, layer_input, doc_lens):
        tok_rows = queries.shape[1]
        kv_width = keys.shape[2]
        heads_kv = kv_width // HD
        group = queries.shape[2] // kv_width
        inverse = 1.0 / math.sqrt(HD)
        blocks_back = min(8, n_context // 4)

        owned = D // (n_data * n_context)
        token_rows = layer_input[0].reshape(tok_rows, n_data, n_cz, n_cw, owned)
        column_share = lax.all_to_all(token_rows, "cw", split_axis=3, concat_axis=0, tiled=True)
        column_share = column_share.reshape(tok_rows * n_cw, n_data * n_cz * owned)

        own_pair = jnp.concatenate([keys[0], values[0]], axis=1)
        earlier = [shifted(own_pair, d, n_context) for d in range(blocks_back, 0, -1)]
        window_pair = jnp.concatenate(earlier + [own_pair], axis=0)
        span = window_pair.shape[0]
        key_win = window_pair[:, :kv_width].reshape(span, heads_kv, HD)
        value_win = window_pair[:, kv_width:].reshape(span, heads_kv, HD)
        device = lax.axis_index("cz") * n_cw + lax.axis_index("cw")
        query_pos = device * tok_rows + jnp.arange(tok_rows, dtype=jnp.int32)
        key_pos = (device - blocks_back) * tok_rows + jnp.arange(span, dtype=jnp.int32)
        query_ids = doc_index(doc_lens[0], query_pos)
        key_ids = doc_index(doc_lens[0], key_pos)
        allowed = (
            (key_pos[None, :] <= query_pos[:, None])
            & (key_ids[None, :] == query_ids[:, None])
            & (key_pos[None, :] >= 0)
        )
        query_blk = queries[0].reshape(tok_rows, heads_kv, group, HD)
        grad_blk = out_grad[0].reshape(tok_rows, heads_kv, group, HD)
        scores = (
            jnp.einsum("ighd,jgd->ghij", query_blk, key_win, preferred_element_type=jnp.float32)
            * inverse
        )
        scores = jnp.where(allowed[None, None], scores, NEGATIVE)
        peak = jnp.max(scores, axis=-1, keepdims=True)
        exponent = jnp.exp(scores - peak)
        probs = exponent / jnp.sum(exponent, axis=-1, keepdims=True)
        probs_half = probs.astype(jnp.bfloat16)
        output = jnp.einsum("ghij,jgd->ighd", probs_half, value_win, preferred_element_type=jnp.float32)
        out_half = output.astype(jnp.bfloat16)
        delta = jnp.einsum("ighd,ighd->ghi", grad_blk, out_half, preferred_element_type=jnp.float32)
        prob_grad = jnp.einsum(
            "ighd,jgd->ghij", grad_blk, value_win, preferred_element_type=jnp.float32
        )
        score_grad = (probs * (prob_grad - delta[..., None])).astype(jnp.bfloat16)
        query_part = (
            jnp.einsum("ghij,jgd->ighd", score_grad, key_win, preferred_element_type=jnp.float32)
            * inverse
        ).astype(jnp.bfloat16)
        key_part = (
            jnp.einsum("ghij,ighd->jgd", score_grad, query_blk, preferred_element_type=jnp.float32)
            * inverse
        )
        value_part = jnp.einsum(
            "ghij,ighd->jgd", probs_half, grad_blk, preferred_element_type=jnp.float32
        )
        pair_grad = jnp.concatenate(
            [key_part.reshape(span, kv_width), value_part.reshape(span, kv_width)], axis=1
        )

        def block_back(distance):
            first_row = (blocks_back - distance) * tok_rows
            return pair_grad[first_row : first_row + tok_rows]

        total = block_back(0)
        for distance in range(1, blocks_back + 1):
            total = total + shifted(block_back(distance), -distance, n_context)
        pair_half = total.astype(jnp.bfloat16)

        grad_scale = 1.0 / math.sqrt(tok_rows * n_context * n_data)
        group_grad = lax.all_gather(pair_half, "cw", axis=0, tiled=True)
        batch_grad = lax.dot_general(
            column_share,
            group_grad,
            (((0,), (0,)), ((), ())),
            preferred_element_type=jnp.float32,
        )
        weight_grad = lax.psum_scatter(
            batch_grad * grad_scale, ("dp", "cz"), scatter_dimension=0, tiled=True
        )
        attn_out = out_half.reshape(tok_rows, group * kv_width)[None]
        query_grad = query_part.reshape(tok_rows, group * kv_width)[None]
        key_grad = pair_half[:, :kv_width][None]
        value_grad = pair_half[:, kv_width:][None]
        return (attn_out, query_grad, key_grad, value_grad, weight_grad)

    return shards


def solution(mesh):
    n_data = mesh.shape["dp"]
    n_context = mesh.shape["ctx"]
    n_cw = 8 if n_context % 8 == 0 else n_context
    n_cz = n_context // n_cw
    split = Mesh(mesh.devices.reshape(n_data, n_cz, n_cw), ("dp", "cz", "cw"))
    tokens = P("dp", CTX, None)
    in_specs = (tokens, tokens, tokens, tokens, tokens, P("dp", None))
    out_specs = (tokens, tokens, tokens, tokens, P(("dp", "cz", "cw"), None))
    return jax.shard_map(
        make_shards(n_data, n_cz, n_cw),
        mesh=split,
        in_specs=in_specs,
        out_specs=out_specs,
        check_vma=False,
    )
```

time: 714 us -> 593 us (0.83)
  waiting for transfers between devices: 507 us -> 420 us
  starting transfers between devices: 104 us -> 54.2 us
  blocking collectives: 12.8 us -> 33 us
    all_gather x1, waiting for transfers between devices: 337 us -> 26.9 us  [shards(): group_grad = lax.all_gather(pair_half, 'cw', axis=0, tiled=True)]
    unnamed x2 -> x3, waiting for transfers between devices: 4.45 us -> 268 us
    all_to_all x1 -> x0, starting transfers between devices: 35 us -> none  [shards(): lax.all_to_all(split_rows, 'ctx', split_axis=2, concat_axis=0, tiled=True)]
    all_to_all x0 -> x1, blocking collectives: none -> 33 us  [shards(): lax.all_to_all(token_rows, 'cw', split_axis=3, concat_axis=0, tiled=True)]
    ppermute x16, waiting for transfers between devices: 149 us -> 126 us  [shifted(): return lax.ppermute(block, CTX, route)]
    all_to_all x1 -> x0, waiting for transfers between devices: 15.4 us -> none  [shards(): lax.all_to_all(split_rows, 'ctx', split_axis=2, concat_axis=0, tiled=True)]
    unnamed x1 -> x0, blocking collectives: 12.8 us -> none
    ppermute x16, starting transfers between devices: 66.9 us -> 54.2 us  [shifted(): return lax.ppermute(block, CTX, route)]
  transfers between devices with their start and end apart: 19 -> 18, of which waited for: 19 -> 13; matrix products, arithmetic and copies ran while one was open for 3% -> 3% of each run, Pallas kernels for 0% -> 0%
where the time goes in v1:
time: 593 us; the launch traced here: 591 us
  waiting for transfers between devices  420 us (71%)
  starting transfers between devices  54.2 us (9%)
  matrix products  33.1 us (6%)
  blocking collectives  33 us (6%)
  local copies, waits for them, and re-layouts  23.2 us (4%)
  between operations  15.1 us (3%)
  other arithmetic  11.4 us (2%)
    unnamed x3, waiting for transfers between devices  268 us
    ppermute x16, waiting for transfers between devices, shifted(): return lax.ppermute(block, CTX, route)  126 us
    ppermute x16, starting transfers between devices, shifted(): return lax.ppermute(block, CTX, route)  54.2 us
    all_to_all x1, blocking collectives, shards(): lax.all_to_all(token_rows, 'cw', split_axis=3, concat_axis=0, tiled=True)  33 us
    all_gather x1, waiting for transfers between devices, shards(): group_grad = lax.all_gather(pair_half, 'cw', axis=0, tiled=True)  26.9 us
    unnamed x44, local copies, waits for them, and re-layouts  12.7 us
  transfers between devices with their start and end apart: 18, of which 13 were waited for; matrix products, arithmetic and copies ran while one was open for 3% of the time, Pallas kernels for 0%

profile of v1, /device:TPU:38, one launch (start us, length us, event | category | flops | bytes accessed | tf_op | source)
XLA Modules:
  0.0 590.6 jit_solution(1896691711848036301)
XLA Ops:
  9.4 3.8 collective-permute-start.7
  13.1 3.5 collective-permute-start.6
  16.6 4.9 collective-permute-start.2
  21.5 3.4 collective-permute-start.1
  25.0 5.0 collective-permute-start
  31.2 1.9 and_and_fusion
  36.0 11.6 %collective-permute-start.3 = (bf16[128,1024]{0,1:T(8,128)(2,1)S(1)}, bf16[128,1024]{0,1:T(8,128)(2,1)S(1)}, u32[]{:S(2)}, u32[]{:S(2)}) collective-permute-start(bf16[128,1024]{0,1:T(8,128)(2,1)S(1)} %pad_maximum_fusion.1), channel_id=1, source_target_pairs={{0,5},{1,6},{2,7},{3,8},{4,9},{5,10},{6,11},{7,12},{8,13},{9,14},{... | collective-permute-start | bytes 786440 | tf_op jit(solution)/shard_map/ppermute | solution.py:19
  50.6 2.1 collective-permute-start.5
  53.8 12.0 %collective-permute-done.4 = bf16[128,1024]{0,1:T(8,128)(2,1)S(1)} collective-permute-done((bf16[128,1024]{0,1:T(8,128)(2,1)S(1)}, bf16[128,1024]{0,1:T(8,128)(2,1)S(1)}, u32[]{:S(2)}, u32[]{:S(2)}) %collective-permute-start.4) | collective-permute-done | bytes 262176 | tf_op jit(solution)/shard_map/ppermute | solution.py:19
  68.9 6.9 %fusion.35 = (f32[4,5,128]{2,1,0:T(8,128)S(1)}, f32[4,5,128,1152]{2,3,1,0:T(8,128)}) fusion(pred[128,1152]{0,1:T(8,128)(4,1)S(1)} %copy-done.11, bf16[1152,4,128,1]{0,2,3,1:T(8,128)(2,1)S(1)} %bitcast.102, bf16[128,4,5,128]{0,3,2,1:T(8,128)(2,1)S(1)} %bitcast.105), kind=kOutput, calls=%fused_computation.79 | convolution fusion | flops 766772352 | bytes 13789184 | tf_op jit(solution)/shard_map/sub | solution.py:67
  75.8 5.9 fusion.7
  81.7 3.3 fusion.36
  84.9 2.0 copy.83
  87.0 5.2 fusion.14
  92.2 5.6 fusion.2
  97.8 3.3 fusion.8
  101.1 3.1 copy.82
  104.2 2.0 fusion.25
  106.3 4.3 collective-permute-start.8
  112.5 2.1 collective-permute-start.10
  118.5 40.6 %collective-permute-done.8 = f32[128,1024]{1,0:T(8,128)S(1)} collective-permute-done((f32[128,1024]{1,0:T(8,128)S(1)}, f32[128,1024]{1,0:T(8,128)S(1)}, u32[]{:S(2)}, u32[]{:S(2)}) %collective-permute-start.8) | collective-permute-done | bytes 524320 | tf_op jit(solution)/shard_map/ppermute | solution.py:19
  162.9 3.3 collective-permute-done.10
  168.1 18.9 %collective-permute-done.11 = f32[128,1024]{1,0:T(8,128)S(1)} collective-permute-done((f32[128,1024]{1,0:T(8,128)S(1)}, f32[128,1024]{1,0:T(8,128)S(1)}, u32[]{:S(2)}, u32[]{:S(2)}) %collective-permute-start.11) | collective-permute-done | bytes 524320 | tf_op jit(solution)/shard_map/ppermute | solution.py:19
  187.0 15.6 %collective-permute-done.12 = f32[128,1024]{1,0:T(8,128)S(1)} collective-permute-done((f32[128,1024]{1,0:T(8,128)S(1)}, f32[128,1024]{1,0:T(8,128)S(1)}, u32[]{:S(2)}, u32[]{:S(2)}) %collective-permute-start.12) | collective-permute-done | bytes 524320 | tf_op jit(solution)/shard_map/ppermute | solution.py:19
  202.6 11.2 %collective-permute-done.13 = f32[128,1024]{1,0:T(8,128)S(1)} collective-permute-done((f32[128,1024]{1,0:T(8,128)S(1)}, f32[128,1024]{1,0:T(8,128)S(1)}, u32[]{:S(2)}, u32[]{:S(2)}) %collective-permute-start.13) | collective-permute-done | bytes 524320 | tf_op jit(solution)/shard_map/ppermute | solution.py:19
  213.8 13.7 %collective-permute-done.15 = f32[128,1024]{1,0:T(8,128)S(1)} collective-permute-done((f32[128,1024]{1,0:T(8,128)S(1)}, f32[128,1024]{1,0:T(8,128)S(1)}, u32[]{:S(2)}, u32[]{:S(2)}) %collective-permute-start.15) | collective-permute-done | bytes 524320 | tf_op jit(solution)/shard_map/ppermute | solution.py:19
  227.6 7.0 %collective-permute-done.14 = f32[128,1024]{1,0:T(8,128)S(1)} collective-permute-done((f32[128,1024]{1,0:T(8,128)S(1)}, f32[128,1024]{1,0:T(8,128)S(1)}, u32[]{:S(2)}, u32[]{:S(2)}) %collective-permute-start.14) | collective-permute-done | bytes 524320 | tf_op jit(solution)/shard_map/ppermute | solution.py:19
  239.3 33.0 %all_to_all.15 = bf16[128,4,8,8,20]{0,2,4,1,3:T(8,128)(2,1)S(1)} all-to-all(bf16[128,4,8,8,20]{0,2,4,1,3:T(8,128)(2,1)S(1)} %copy.85), channel_id=1, replica_groups=mesh['dp'=4,'cz'=8,'cw'=8] {'cw'}, dimensions={3} | all-to-all | bytes 2621440 | tf_op jit(solution)/shard_map/all_to_all | solution.py:40
  273.1 26.9 %all-gather.2.cloned.1.call-done = bf16[1024,1024]{1,0:T(8,128)(2,1)} async-done(((bf16[128,1024]{1,0:T(8,128)(2,1)}), bf16[1024,1024]{1,0:T(8,128)(2,1)}) %all-gather.2.cloned.1.call-update) | async-done | bytes 2097168 | tf_op jit(solution)/shard_map/all_gather | solution.py:102
  300.0 5.0 multiply_bitcast_fusion
  306.9 3.9 fusion.11
  313.8 267.7 %all-reduce.3.cloned.1.call-done = f32[640,1024]{0,1:T(8,128)} async-done(((f32[640,1024]{0,1:T(8,128)}), f32[640,1024]{0,1:T(8,128)}) %all-reduce.3.cloned.1.call-update) | async-done | bytes 2621456
  (79 shorter events, 36.7 us)
Async XLA Ops:
  7.2 27.4 %copy-start.10 = (bf16[1,128,2560]{2,1,0:T(8,128)(2,1)S(1)}, bf16[1,128,2560]{2,1,0:T(8,128)(2,1)}, u32[]{:S(2)}) copy-start(bf16[1,128,2560]{2,1,0:T(8,128)(2,1)} %param.6) | copy-start | bytes 1966084
  7.2 292.8 %all-gather.2.cloned.1.call-start = ((), (), s32[]{:S(2)}) async-start(), calls=%async_computation.1 | async-start | bytes 2359296 | tf_op jit(solution)/shard_map/all_gather | solution.py:102
  9.4 58.1 %collective-permute-start.7 = (bf16[128,1024]{0,1:T(8,128)(2,1)S(1)}, bf16[128,1024]{0,1:T(8,128)(2,1)S(1)}, u32[]{:S(2)}, u32[]{:S(2)}) collective-permute-start(bf16[128,1024]{0,1:T(8,128)(2,1)S(1)} %pad_maximum_fusion.1), channel_id=1, source_target_pairs={{0,1},{1,2},{2,3},{3,4},{4,5},{5,6},{6,7},{7,8},{8,9},{9,10},{10,1... | collective-permute-start | bytes 786440 | tf_op jit(solution)/shard_map/ppermute | solution.py:19
  13.1 54.3 %collective-permute-start.6 = (bf16[128,1024]{0,1:T(8,128)(2,1)S(1)}, bf16[128,1024]{0,1:T(8,128)(2,1)S(1)}, u32[]{:S(2)}, u32[]{:S(2)}) collective-permute-start(bf16[128,1024]{0,1:T(8,128)(2,1)S(1)} %pad_maximum_fusion.1), channel_id=1, source_target_pairs={{0,2},{1,3},{2,4},{3,5},{4,6},{5,7},{6,8},{7,9},{8,10},{9,11},{10,... | collective-permute-start | bytes 786440 | tf_op jit(solution)/shard_map/ppermute | solution.py:19
  16.6 34.0 %collective-permute-start.2 = (bf16[128,1024]{0,1:T(8,128)(2,1)S(1)}, bf16[128,1024]{0,1:T(8,128)(2,1)S(1)}, u32[]{:S(2)}, u32[]{:S(2)}) collective-permute-start(bf16[128,1024]{0,1:T(8,128)(2,1)S(1)} %pad_maximum_fusion.1), channel_id=1, source_target_pairs={{0,6},{1,7},{2,8},{3,9},{4,10},{5,11},{6,12},{7,13},{8,14},{9,15},... | collective-permute-start | bytes 786440 | tf_op jit(solution)/shard_map/ppermute | solution.py:19
  21.5 27.0 %collective-permute-start.1 = (bf16[128,1024]{0,1:T(8,128)(2,1)S(1)}, bf16[128,1024]{0,1:T(8,128)(2,1)S(1)}, u32[]{:S(2)}, u32[]{:S(2)}) collective-permute-start(bf16[128,1024]{0,1:T(8,128)(2,1)S(1)} %pad_maximum_fusion.1), channel_id=1, source_target_pairs={{0,7},{1,8},{2,9},{3,10},{4,11},{5,12},{6,13},{7,14},{8,15},{9,16}... | collective-permute-start | bytes 786440 | tf_op jit(solution)/shard_map/ppermute | solution.py:19
  25.0 11.0 %collective-permute-start = (bf16[128,1024]{0,1:T(8,128)(2,1)S(1)}, bf16[128,1024]{0,1:T(8,128)(2,1)}, u32[]{:S(2)}, u32[]{:S(2)}) collective-permute-start(bf16[128,1024]{0,1:T(8,128)(2,1)S(1)} %pad_maximum_fusion.1), channel_id=1, source_target_pairs={{0,8},{1,9},{2,10},{3,11},{4,12},{5,13},{6,14},{7,15},{8,16},{9,17... | collective-permute-start | bytes 786440 | tf_op jit(solution)/shard_map/ppermute | solution.py:19
  34.9 34.0 %copy-start.7 = (bf16[1,128,2560]{1,2,0:T(8,128)(2,1)}, bf16[1,128,2560]{1,2,0:T(8,128)(2,1)S(1)}, u32[]{:S(2)}) copy-start(bf16[1,128,2560]{1,2,0:T(8,128)(2,1)S(1)} %copy.72) | copy-start | bytes 1966084
  36.0 17.8 %collective-permute-start.3 = (bf16[128,1024]{0,1:T(8,128)(2,1)S(1)}, bf16[128,1024]{0,1:T(8,128)(2,1)S(1)}, u32[]{:S(2)}, u32[]{:S(2)}) collective-permute-start(bf16[128,1024]{0,1:T(8,128)(2,1)S(1)} %pad_maximum_fusion.1), channel_id=1, source_target_pairs={{0,5},{1,6},{2,7},{3,8},{4,9},{5,10},{6,11},{7,12},{8,13},{9,14},{... | collective-permute-start | bytes 786440 | tf_op jit(solution)/shard_map/ppermute | solution.py:19
  48.6 17.3 %collective-permute-start.4 = (bf16[128,1024]{0,1:T(8,128)(2,1)S(1)}, bf16[128,1024]{0,1:T(8,128)(2,1)S(1)}, u32[]{:S(2)}, u32[]{:S(2)}) collective-permute-start(bf16[128,1024]{0,1:T(8,128)(2,1)S(1)} %pad_maximum_fusion.1), channel_id=1, source_target_pairs={{0,4},{1,5},{2,6},{3,7},{4,8},{5,9},{6,10},{7,11},{8,12},{9,13},{1... | collective-permute-start | bytes 786440 | tf_op jit(solution)/shard_map/ppermute | solution.py:19
  50.6 16.7 %collective-permute-start.5 = (bf16[128,1024]{0,1:T(8,128)(2,1)S(1)}, bf16[128,1024]{0,1:T(8,128)(2,1)S(1)}, u32[]{:S(2)}, u32[]{:S(2)}) collective-permute-start(bf16[128,1024]{0,1:T(8,128)(2,1)S(1)} %pad_maximum_fusion.1), channel_id=1, source_target_pairs={{0,3},{1,4},{2,5},{3,6},{4,7},{5,8},{6,9},{7,10},{8,11},{9,12},{10... | collective-permute-start | bytes 786440 | tf_op jit(solution)/shard_map/ppermute | solution.py:19
  67.6 1.3 copy-start.11
  68.9 6.9 %copy-start.4 = (bf16[1152,512]{0,1:T(8,128)(2,1)}, bf16[1152,512]{0,1:T(8,128)(2,1)S(1)}, u32[]{:S(2)}) copy-start(bf16[1152,512]{0,1:T(8,128)(2,1)S(1)} %get-tuple-element.33) | copy-start | bytes 3538948
  81.7 3.3 copy-start
  87.0 5.2 copy-start.3
  92.2 5.6 copy-start.8
  97.8 3.3 copy-start.1
  104.2 130.3 %copy-start.2 = (f32[1152,512]{1,0:T(8,128)S(1)}, f32[1152,512]{1,0:T(8,128)}, u32[]{:S(2)}) copy-start(f32[1152,512]{1,0:T(8,128)} %copy.82) | copy-start | bytes 7077892
  106.3 52.8 %collective-permute-start.8 = (f32[128,1024]{1,0:T(8,128)S(1)}, f32[128,1024]{1,0:T(8,128)S(1)}, u32[]{:S(2)}, u32[]{:S(2)}) collective-permute-start(f32[128,1024]{1,0:T(8,128)S(1)} %get-tuple-element.25), channel_id=1, source_target_pairs={{1,0},{2,1},{3,2},{4,3},{5,4},{6,5},{7,6},{8,7},{9,8},{10,9},{11,1... | collective-permute-start | bytes 1572872 | tf_op jit(solution)/shard_map/ppermute | solution.py:19
  110.6 50.4 %collective-permute-start.9 = (f32[128,1024]{1,0:T(8,128)S(1)}, f32[128,1024]{1,0:T(8,128)S(1)}, u32[]{:S(2)}, u32[]{:S(2)}) collective-permute-start(f32[128,1024]{1,0:T(8,128)S(1)} %get-tuple-element.26), channel_id=1, source_target_pairs={{2,0},{3,1},{4,2},{5,3},{6,4},{7,5},{8,6},{9,7},{10,8},{11,9},{12,... | collective-permute-start | bytes 1572872 | tf_op jit(solution)/shard_map/ppermute | solution.py:19
  112.5 53.7 %collective-permute-start.10 = (f32[128,1024]{1,0:T(8,128)S(1)}, f32[128,1024]{1,0:T(8,128)S(1)}, u32[]{:S(2)}, u32[]{:S(2)}) collective-permute-start(f32[128,1024]{1,0:T(8,128)S(1)} %get-tuple-element.27), channel_id=1, source_target_pairs={{3,0},{4,1},{5,2},{6,3},{7,4},{8,5},{9,6},{10,7},{11,8},{12,9},{13... | collective-permute-start | bytes 1572872 | tf_op jit(solution)/shard_map/ppermute | solution.py:19
  114.6 72.4 %collective-permute-start.11 = (f32[128,1024]{1,0:T(8,128)S(1)}, f32[128,1024]{1,0:T(8,128)S(1)}, u32[]{:S(2)}, u32[]{:S(2)}) collective-permute-start(f32[128,1024]{1,0:T(8,128)S(1)} %get-tuple-element.28), channel_id=1, source_target_pairs={{4,0},{5,1},{6,2},{7,3},{8,4},{9,5},{10,6},{11,7},{12,8},{13,9},{1... | collective-permute-start | bytes 1572872 | tf_op jit(solution)/shard_map/ppermute | solution.py:19
  116.5 86.1 %collective-permute-start.12 = (f32[128,1024]{1,0:T(8,128)S(1)}, f32[128,1024]{1,0:T(8,128)S(1)}, u32[]{:S(2)}, u32[]{:S(2)}) collective-permute-start(f32[128,1024]{1,0:T(8,128)S(1)} %get-tuple-element.29), channel_id=1, source_target_pairs={{5,0},{6,1},{7,2},{8,3},{9,4},{10,5},{11,6},{12,7},{13,8},{14,9},{... | collective-permute-start | bytes 1572872 | tf_op jit(solution)/shard_map/ppermute | solution.py:19
  159.0 54.8 %collective-permute-start.13 = (f32[128,1024]{1,0:T(8,128)S(1)}, f32[128,1024]{1,0:T(8,128)S(1)}, u32[]{:S(2)}, u32[]{:S(2)}) collective-permute-start(f32[128,1024]{1,0:T(8,128)S(1)} %get-tuple-element.30), channel_id=1, source_target_pairs={{6,0},{7,1},{8,2},{9,3},{10,4},{11,5},{12,6},{13,7},{14,8},{15,9},... | collective-permute-start | bytes 1572872 | tf_op jit(solution)/shard_map/ppermute | solution.py:19
  160.9 66.6 %collective-permute-start.15 = (f32[128,1024]{1,0:T(8,128)S(1)}, f32[128,1024]{1,0:T(8,128)S(1)}, u32[]{:S(2)}, u32[]{:S(2)}) collective-permute-start(f32[128,1024]{1,0:T(8,128)S(1)} %get-tuple-element.31), channel_id=1, source_target_pairs={{8,0},{9,1},{10,2},{11,3},{12,4},{13,5},{14,6},{15,7},{16,8},{17,9... | collective-permute-start | bytes 1572872 | tf_op jit(solution)/shard_map/ppermute | solution.py:19
  166.2 68.3 %collective-permute-start.14 = (f32[128,1024]{1,0:T(8,128)S(1)}, f32[128,1024]{1,0:T(8,128)S(1)}, u32[]{:S(2)}, u32[]{:S(2)}) collective-permute-start(f32[128,1024]{1,0:T(8,128)S(1)} %get-tuple-element.32), channel_id=1, source_target_pairs={{7,0},{8,1},{9,2},{10,3},{11,4},{12,5},{13,6},{14,7},{15,8},{16,9}... | collective-permute-start | bytes 1572872 | tf_op jit(solution)/shard_map/ppermute | solution.py:19
  235.7 345.8 %all-reduce.3.cloned.1.call-start = ((), (), s32[]{:S(2)}) async-start(), calls=%async_computation.2 | async-start | bytes 5242880
  305.0 0.7 copy-start.12
  305.0 1.9 copy-start.5
  306.9 5.1 copy-start.6
  310.9 2.2 copy-start.9
Sparse Core Ops, SparseCore 0:
  235.8 64.1 all-gather.1
  305.1 276.3 all-reduce.2

commit v2 on v1

--- a/solution.py
+++ b/solution.py
@@ -36,9 +36,15 @@
         blocks_back = min(8, n_context // 4)
 
         owned = D // (n_data * n_context)
-        token_rows = layer_input[0].reshape(tok_rows, n_data, n_cz, n_cw, owned)
-        column_share = lax.all_to_all(token_rows, "cw", split_axis=3, concat_axis=0, tiled=True)
-        column_share = column_share.reshape(tok_rows * n_cw, n_data * n_cz * owned)
+        member = lax.axis_index("cw")
+        chunks = layer_input[0].reshape(tok_rows, n_data, n_cz, n_cw, owned)
+        chunks = chunks.transpose(3, 0, 2, 1, 4).reshape(n_cw, tok_rows, n_cz * n_data * owned)
+        received = [lax.dynamic_index_in_dim(chunks, member, 0, keepdims=False)]
+        for k in range(1, n_cw):
+            route = [(i, (i + k) % n_cw) for i in range(n_cw)]
+            outgoing = lax.dynamic_index_in_dim(chunks, (member + k) % n_cw, 0, keepdims=False)
+            received.append(lax.ppermute(outgoing, "cw", route))
+        column_share = jnp.concatenate(received[::-1], axis=0)
 
         own_pair = jnp.concatenate([keys[0], values[0]], axis=1)
         earlier = [shifted(own_pair, d, n_context) for d in range(blocks_back, 0, -1)]
@@ -100,15 +106,20 @@
 
         grad_scale = 1.0 / math.sqrt(tok_rows * n_context * n_data)
         group_grad = lax.all_gather(pair_half, "cw", axis=0, tiled=True)
+        group_grad = lax.dynamic_slice_in_dim(
+            jnp.concatenate([group_grad, group_grad], axis=0),
+            ((member + 1) % n_cw) * tok_rows,
+            n_cw * tok_rows,
+            0,
+        )
         batch_grad = lax.dot_general(
             column_share,
             group_grad,
             (((0,), (0,)), ((), ())),
             preferred_element_type=jnp.float32,
         )
-        weight_grad = lax.psum_scatter(
-            batch_grad * grad_scale, ("dp", "cz"), scatter_dimension=0, tiled=True
-        )
+        by_layer = lax.psum_scatter(batch_grad * grad_scale, "cz", scatter_dimension=0, tiled=True)
+        weight_grad = lax.psum_scatter(by_layer, "dp", scatter_dimension=0, tiled=True)
         attn_out = out_half.reshape(tok_rows, group * kv_width)[None]
         query_grad = query_part.reshape(tok_rows, group * kv_width)[None]
         key_grad = pair_half[:, :kv_width][None]

time: 593 us -> 380 us (0.64)
  waiting for transfers between devices: 420 us -> 201 us
  blocking collectives: 33 us -> 11.8 us
  starting transfers between devices: 54.2 us -> 70.8 us
  local copies, waits for them, and re-layouts: 23.2 us -> 33.4 us
    unnamed x3, waiting for transfers between devices: 268 us -> 4.47 us
    reduce_scatter x0 -> x1, waiting for transfers between devices: none -> 36 us  [shards(): lax.psum_scatter(batch_grad * grad_scale, 'cz', scatter_dimension=0, tile...]
    all_to_all x1 -> x0, blocking collectives: 33 us -> none  [shards(): lax.all_to_all(token_rows, 'cw', split_axis=3, concat_axis=0, tiled=True)]
    ppermute x0 -> x7, starting transfers between devices: none -> 14.7 us  [shards(): received.append(lax.ppermute(outgoing, 'cw', route))]
    unnamed x0 -> x1, blocking collectives: none -> 11.8 us
    ppermute x0 -> x7, waiting for transfers between devices: none -> 10.8 us  [shards(): received.append(lax.ppermute(outgoing, 'cw', route))]
    dynamic_slice x0 -> x9, local copies, waits for them, and re-layouts: none -> 8.26 us  [the longest x7 4.51 us: shards(): lax.dynamic_index_in_dim(chunks, (member + k) % n_cw, 0, keepdims=False)]
    unnamed x44 -> x52, local copies, waits for them, and re-layouts: 12.7 us -> 16.1 us
  transfers between devices with their start and end apart: 18 -> 26, of which waited for: 13 -> 17; matrix products, arithmetic and copies ran while one was open for 3% -> 8% of each run, Pallas kernels for 0% -> 0%
where the time goes in v2:
time: 380 us; the launch traced here: 377 us
  waiting for transfers between devices  201 us (53%)
  starting transfers between devices  70.8 us (19%)
  local copies, waits for them, and re-layouts  33.4 us (9%)
  matrix products  33.2 us (9%)
  between operations  15.4 us (4%)
  blocking collectives  11.8 us (3%)
  other arithmetic  11.4 us (3%)
    ppermute x16, waiting for transfers between devices, shifted(): return lax.ppermute(block, CTX, route)  126 us
    ppermute x16, starting transfers between devices, shifted(): return lax.ppermute(block, CTX, route)  54.2 us
    reduce_scatter x1, waiting for transfers between devices, shards(): lax.psum_scatter(batch_grad * grad_scale, 'cz', scatter_dimension=0, tile...  36 us
    all_gather x1, waiting for transfers between devices, shards(): group_grad = lax.all_gather(pair_half, 'cw', axis=0, tiled=True)  24.4 us
    unnamed x52, local copies, waits for them, and re-layouts  16.1 us
    ppermute x7, starting transfers between devices, shards(): received.append(lax.ppermute(outgoing, 'cw', route))  14.7 us
    unnamed x1, blocking collectives  11.8 us
    ppermute x7, waiting for transfers between devices, shards(): received.append(lax.ppermute(outgoing, 'cw', route))  10.8 us
  transfers between devices with their start and end apart: 26, of which 17 were waited for; matrix products, arithmetic and copies ran while one was open for 8% of the time, Pallas kernels for 0%

profile of v2, /device:TPU:38, one launch (start us, length us, event | category | flops | bytes accessed | tf_op | source)
XLA Modules:
  0.0 377.5 jit_solution(11318091829829404066)
XLA Ops:
  9.4 3.8 collective-permute-start.7
  13.1 3.5 collective-permute-start.6
  16.6 4.9 %collective-permute-start.2 = (bf16[128,1024]{0,1:T(8,128)(2,1)S(1)}, bf16[128,1024]{0,1:T(8,128)(2,1)S(1)}, u32[]{:S(2)}, u32[]{:S(2)}) collective-permute-start(bf16[128,1024]{0,1:T(8,128)(2,1)S(1)} %pad_maximum_fusion.1), channel_id=1, source_target_pairs={{0,6},{1,7},{2,8},{3,9},{4,10},{5,11},{6,12},{7,13},{8,14},{9,15},... | collective-permute-start | bytes 786440 | tf_op jit(solution)/shard_map/ppermute | solution.py:19
  21.5 3.4 collective-permute-start.1
  25.0 5.0 %collective-permute-start = (bf16[128,1024]{0,1:T(8,128)(2,1)S(1)}, bf16[128,1024]{0,1:T(8,128)(2,1)}, u32[]{:S(2)}, u32[]{:S(2)}) collective-permute-start(bf16[128,1024]{0,1:T(8,128)(2,1)S(1)} %pad_maximum_fusion.1), channel_id=1, source_target_pairs={{0,8},{1,9},{2,10},{3,11},{4,12},{5,13},{6,14},{7,15},{8,16},{9,17... | collective-permute-start | bytes 786440 | tf_op jit(solution)/shard_map/ppermute | solution.py:19
  36.0 11.6 %collective-permute-start.3 = (bf16[128,1024]{0,1:T(8,128)(2,1)S(1)}, bf16[128,1024]{0,1:T(8,128)(2,1)S(1)}, u32[]{:S(2)}, u32[]{:S(2)}) collective-permute-start(bf16[128,1024]{0,1:T(8,128)(2,1)S(1)} %pad_maximum_fusion.1), channel_id=1, source_target_pairs={{0,5},{1,6},{2,7},{3,8},{4,9},{5,10},{6,11},{7,12},{8,13},{9,14},{... | collective-permute-start | bytes 786440 | tf_op jit(solution)/shard_map/ppermute | solution.py:19
  53.8 12.0 %collective-permute-done.4 = bf16[128,1024]{0,1:T(8,128)(2,1)S(1)} collective-permute-done((bf16[128,1024]{0,1:T(8,128)(2,1)S(1)}, bf16[128,1024]{0,1:T(8,128)(2,1)S(1)}, u32[]{:S(2)}, u32[]{:S(2)}) %collective-permute-start.4) | collective-permute-done | bytes 262176 | tf_op jit(solution)/shard_map/ppermute | solution.py:19
  68.9 6.9 %fusion.42 = (f32[4,5,128]{2,1,0:T(8,128)S(1)}, f32[4,5,128,1152]{2,3,1,0:T(8,128)}) fusion(pred[128,1152]{0,1:T(8,128)(4,1)S(1)} %copy-done.11, bf16[1152,4,128,1]{0,2,3,1:T(8,128)(2,1)S(1)} %bitcast.102, bf16[128,4,5,128]{0,3,2,1:T(8,128)(2,1)S(1)} %bitcast.105), kind=kOutput, calls=%fused_computation.99 | convolution fusion | flops 766772352 | bytes 13789184 | tf_op jit(solution)/shard_map/sub | solution.py:73
  75.8 5.9 %fusion.8 = bf16[4,5,128,1152]{2,3,1,0:T(8,128)(2,1)S(1)} fusion(f32[4,5,128,1152]{2,3,1,0:T(8,128)} %get-tuple-element.51, f32[4,5,128]{2,1,0:T(8,128)S(1)} %get-tuple-element.50), kind=kLoop, calls=%fused_computation.27 | loop fusion | flops 5898240 | bytes 17704960 | tf_op jit(solution)/shard_map/convert_element_type | solution.py:75
  81.7 3.2 fusion.43
  87.0 5.2 %fusion.19 = (f32[4,5,128]{2,1,0:T(8,128)S(1)}, bf16[4,128,5,128]{3,1,2,0:T(8,128)(2,1)}) fusion(bf16[4,5,128,128]{2,3,1,0:T(8,128)(2,1)S(1)} %bitcast.98, bf16[1152,4,128,1]{0,2,3,1:T(8,128)(2,1)} %bitcast.100, bf16[4,5,128,1152]{2,3,1,0:T(8,128)(2,1)} %copy-done), kind=kOutput, calls=%fused_computation.40 | convolution fusion | flops 756610560 | bytes 8398848 | tf_op jit(solution)/shard_map/ghij,jgd->ighd/dot_general | solution.py:76
  92.2 5.6 %fusion.3 = bf16[4,5,128,1152]{2,3,1,0:T(8,128)(2,1)S(1)} fusion(bf16[1152,4,128,1]{0,2,3,1:T(8,128)(2,1)S(1)} %bitcast.101, bf16[128,4,5,128]{0,3,2,1:T(8,128)(2,1)S(1)} %bitcast.99, f32[4,5,128]{2,1,0:T(8,128)S(1)} %get-tuple-element.52, f32[4,5,128,1152]{2,3,1,0:T(8,128)} %get-tuple-element.51, f32[4,5,128]{2,1,0:T(8,128)S(1)} %get-tuple-element.50), kind=kOutput, calls=%fused_computation.3 | convolution fusion | flops 766771200 | bytes 19550208 | tf_op jit(solution)/shard_map/ighd,jgd->ghij/dot_general | solution.py:79
  97.8 3.3 fusion.9
  106.2 4.3 %collective-permute-start.8 = (f32[128,1024]{1,0:T(8,128)S(1)}, f32[128,1024]{1,0:T(8,128)S(1)}, u32[]{:S(2)}, u32[]{:S(2)}) collective-permute-start(f32[128,1024]{1,0:T(8,128)S(1)} %get-tuple-element.30), channel_id=1, source_target_pairs={{1,0},{2,1},{3,2},{4,3},{5,4},{6,5},{7,6},{8,7},{9,8},{10,9},{11,1... | collective-permute-start | bytes 1572872 | tf_op jit(solution)/shard_map/ppermute | solution.py:19
  118.5 40.6 %collective-permute-done.8 = f32[128,1024]{1,0:T(8,128)S(1)} collective-permute-done((f32[128,1024]{1,0:T(8,128)S(1)}, f32[128,1024]{1,0:T(8,128)S(1)}, u32[]{:S(2)}, u32[]{:S(2)}) %collective-permute-start.8) | collective-permute-done | bytes 524320 | tf_op jit(solution)/shard_map/ppermute | solution.py:19
  162.9 3.3 collective-permute-done.10
  168.1 18.9 %collective-permute-done.11 = f32[128,1024]{1,0:T(8,128)S(1)} collective-permute-done((f32[128,1024]{1,0:T(8,128)S(1)}, f32[128,1024]{1,0:T(8,128)S(1)}, u32[]{:S(2)}, u32[]{:S(2)}) %collective-permute-start.11) | collective-permute-done | bytes 524320 | tf_op jit(solution)/shard_map/ppermute | solution.py:19
  187.0 15.6 %collective-permute-done.12 = f32[128,1024]{1,0:T(8,128)S(1)} collective-permute-done((f32[128,1024]{1,0:T(8,128)S(1)}, f32[128,1024]{1,0:T(8,128)S(1)}, u32[]{:S(2)}, u32[]{:S(2)}) %collective-permute-start.12) | collective-permute-done | bytes 524320 | tf_op jit(solution)/shard_map/ppermute | solution.py:19
  202.6 11.2 %collective-permute-done.13 = f32[128,1024]{1,0:T(8,128)S(1)} collective-permute-done((f32[128,1024]{1,0:T(8,128)S(1)}, f32[128,1024]{1,0:T(8,128)S(1)}, u32[]{:S(2)}, u32[]{:S(2)}) %collective-permute-start.13) | collective-permute-done | bytes 524320 | tf_op jit(solution)/shard_map/ppermute | solution.py:19
  213.8 13.7 %collective-permute-done.15 = f32[128,1024]{1,0:T(8,128)S(1)} collective-permute-done((f32[128,1024]{1,0:T(8,128)S(1)}, f32[128,1024]{1,0:T(8,128)S(1)}, u32[]{:S(2)}, u32[]{:S(2)}) %collective-permute-start.15) | collective-permute-done | bytes 524320 | tf_op jit(solution)/shard_map/ppermute | solution.py:19
  227.5 7.1 %collective-permute-done.14 = f32[128,1024]{1,0:T(8,128)S(1)} collective-permute-done((f32[128,1024]{1,0:T(8,128)S(1)}, f32[128,1024]{1,0:T(8,128)S(1)}, u32[]{:S(2)}, u32[]{:S(2)}) %collective-permute-start.14) | collective-permute-done | bytes 524320 | tf_op jit(solution)/shard_map/ppermute | solution.py:19
  238.2 3.6 constant_dynamic-slice_fusion.1
  245.8 7.5 %collective-permute-start.19 = (bf16[128,640]{1,0:T(8,128)(2,1)S(1)}, bf16[128,640]{1,0:T(8,128)(2,1)S(1)}, u32[]{:S(2)}, u32[]{:S(2)}) collective-permute-start(bf16[128,640]{1,0:T(8,128)(2,1)S(1)} %bitcast.113), channel_id=1, source_target_pairs={{0,4},{1,5},{2,6},{3,7},{4,0},{5,1},{6,2},{7,3},{8,12},{9,13},{10,... | collective-permute-start | bytes 491528 | tf_op jit(solution)/shard_map/ppermute | solution.py:46
  253.5 4.5 %collective-permute-start.20 = (bf16[128,640]{1,0:T(8,128)(2,1)S(1)}, bf16[128,640]{1,0:T(8,128)(2,1)S(1)}, u32[]{:S(2)}, u32[]{:S(2)}) collective-permute-start(bf16[128,640]{1,0:T(8,128)(2,1)S(1)} %bitcast.112), channel_id=1, source_target_pairs={{0,3},{1,4},{2,5},{3,6},{4,7},{5,0},{6,1},{7,2},{8,11},{9,12},{10,... | collective-permute-start | bytes 491528 | tf_op jit(solution)/shard_map/ppermute | solution.py:46
  265.0 5.1 %collective-permute-done.20 = bf16[128,640]{1,0:T(8,128)(2,1)S(1)} collective-permute-done((bf16[128,640]{1,0:T(8,128)(2,1)S(1)}, bf16[128,640]{1,0:T(8,128)(2,1)S(1)}, u32[]{:S(2)}, u32[]{:S(2)}) %collective-permute-start.20) | collective-permute-done | bytes 163872 | tf_op jit(solution)/shard_map/ppermute | solution.py:46
  271.4 4.6 %collective-permute-done.22 = bf16[128,640]{1,0:T(8,128)(2,1)S(1)} collective-permute-done((bf16[128,640]{1,0:T(8,128)(2,1)S(1)}, bf16[128,640]{1,0:T(8,128)(2,1)S(1)}, u32[]{:S(2)}, u32[]{:S(2)}) %collective-permute-start.22) | collective-permute-done | bytes 163872 | tf_op jit(solution)/shard_map/ppermute | solution.py:46
  277.4 24.4 %all-gather.2.cloned.1.call-done = bf16[1024,1024]{1,0:T(8,128)(2,1)} async-done(((bf16[128,1024]{1,0:T(8,128)(2,1)}), bf16[1024,1024]{1,0:T(8,128)(2,1)}) %all-gather.2.cloned.1.call-update) | async-done | bytes 2097168 | tf_op jit(solution)/shard_map/all_gather | solution.py:108
  301.7 5.1 %fusion.15 = f32[640,1024]{1,0:T(8,128)} fusion(bf16[1024,640]{1,0:T(8,128)(2,1)} %bitcast_dynamic-update-slice_fusion, s32[]{:T(128)S(6)} %select_n.81, bf16[1024,1024]{1,0:T(8,128)(2,1)} %all-gather.2.cloned.1.call-done), kind=kOutput, calls=%fused_computation.35 | convolution fusion | flops 1347026944 | bytes 6029316 | tf_op jit(solution)/shard_map/dot_general | solution.py:115
  308.8 3.9 %fusion.18 = bf16[4,128,5,128]{3,1,2,0:T(8,128)(2,1)S(1)} fusion(bf16[1152,4,128,1]{0,2,3,1:T(8,128)(2,1)S(1)} %bitcast.103, bf16[4,5,128,1152]{2,3,1,0:T(8,128)(2,1)} %copy-done.1), kind=kOutput, calls=%fused_computation.37 | convolution fusion | flops 755630080 | bytes 7733248 | tf_op jit(solution)/shard_map/ghij,jgd->ighd/dot_general | solution.py:84
  314.9 36.0 %reduce-scatter.4.cloned.1.call-done = f32[80,1024]{1,0:T(8,128)} async-done(((f32[640,1024]{1,0:T(8,128)}), f32[80,1024]{1,0:T(8,128)}) %reduce-scatter.4.cloned.1.call-update) | async-done | bytes 327696 | tf_op jit(solution)/shard_map/reduce_scatter | solution.py:121
  350.9 11.8 %fusion = f32[24,1024]{1,0:T(8,128)S(1)} fusion(f32[80,1024]{1,0:T(8,128)} %reduce-scatter.4.cloned.1.call-done), kind=kCustom, calls=%all-reduce-scatter | all-reduce-scatter fusion | flops 98305 | bytes 427008
  365.4 4.4 %collective-permute-done.23 = f32[12,1024]{1,0:T(8,128)S(1)} collective-permute-done((f32[12,1024]{1,0:T(8,128)S(1)}, f32[12,1024]{1,0:T(8,128)S(1)}, u32[]{:S(2)}, u32[]{:S(2)}) %collective-permute-start.23) | collective-permute-done | bytes 49184
  (112 shorter events, 62.3 us)
Async XLA Ops:
  7.2 27.4 %copy-start.10 = (bf16[1,128,2560]{2,1,0:T(8,128)(2,1)S(1)}, bf16[1,128,2560]{2,1,0:T(8,128)(2,1)}, u32[]{:S(2)}) copy-start(bf16[1,128,2560]{2,1,0:T(8,128)(2,1)} %param.6) | copy-start | bytes 1966084
  7.2 294.6 %all-gather.2.cloned.1.call-start = ((), (), s32[]{:S(2)}) async-start(), calls=%async_computation.1 | async-start | bytes 2359296 | tf_op jit(solution)/shard_map/all_gather | solution.py:108
  9.4 58.1 %collective-permute-start.7 = (bf16[128,1024]{0,1:T(8,128)(2,1)S(1)}, bf16[128,1024]{0,1:T(8,128)(2,1)S(1)}, u32[]{:S(2)}, u32[]{:S(2)}) collective-permute-start(bf16[128,1024]{0,1:T(8,128)(2,1)S(1)} %pad_maximum_fusion.1), channel_id=1, source_target_pairs={{0,1},{1,2},{2,3},{3,4},{4,5},{5,6},{6,7},{7,8},{8,9},{9,10},{10,1... | collective-permute-start | bytes 786440 | tf_op jit(solution)/shard_map/ppermute | solution.py:19
  13.1 54.3 %collective-permute-start.6 = (bf16[128,1024]{0,1:T(8,128)(2,1)S(1)}, bf16[128,1024]{0,1:T(8,128)(2,1)S(1)}, u32[]{:S(2)}, u32[]{:S(2)}) collective-permute-start(bf16[128,1024]{0,1:T(8,128)(2,1)S(1)} %pad_maximum_fusion.1), channel_id=1, source_target_pairs={{0,2},{1,3},{2,4},{3,5},{4,6},{5,7},{6,8},{7,9},{8,10},{9,11},{10,... | collective-permute-start | bytes 786440 | tf_op jit(solution)/shard_map/ppermute | solution.py:19
  16.6 34.0 %collective-permute-start.2 = (bf16[128,1024]{0,1:T(8,128)(2,1)S(1)}, bf16[128,1024]{0,1:T(8,128)(2,1)S(1)}, u32[]{:S(2)}, u32[]{:S(2)}) collective-permute-start(bf16[128,1024]{0,1:T(8,128)(2,1)S(1)} %pad_maximum_fusion.1), channel_id=1, source_target_pairs={{0,6},{1,7},{2,8},{3,9},{4,10},{5,11},{6,12},{7,13},{8,14},{9,15},... | collective-permute-start | bytes 786440 | tf_op jit(solution)/shard_map/ppermute | solution.py:19
  21.5 27.0 %collective-permute-start.1 = (bf16[128,1024]{0,1:T(8,128)(2,1)S(1)}, bf16[128,1024]{0,1:T(8,128)(2,1)S(1)}, u32[]{:S(2)}, u32[]{:S(2)}) collective-permute-start(bf16[128,1024]{0,1:T(8,128)(2,1)S(1)} %pad_maximum_fusion.1), channel_id=1, source_target_pairs={{0,7},{1,8},{2,9},{3,10},{4,11},{5,12},{6,13},{7,14},{8,15},{9,16}... | collective-permute-start | bytes 786440 | tf_op jit(solution)/shard_map/ppermute | solution.py:19
  25.0 11.0 %collective-permute-start = (bf16[128,1024]{0,1:T(8,128)(2,1)S(1)}, bf16[128,1024]{0,1:T(8,128)(2,1)}, u32[]{:S(2)}, u32[]{:S(2)}) collective-permute-start(bf16[128,1024]{0,1:T(8,128)(2,1)S(1)} %pad_maximum_fusion.1), channel_id=1, source_target_pairs={{0,8},{1,9},{2,10},{3,11},{4,12},{5,13},{6,14},{7,15},{8,16},{9,17... | collective-permute-start | bytes 786440 | tf_op jit(solution)/shard_map/ppermute | solution.py:19
  34.9 34.1 %copy-start.7 = (bf16[1,128,2560]{1,2,0:T(8,128)(2,1)}, bf16[1,128,2560]{1,2,0:T(8,128)(2,1)S(1)}, u32[]{:S(2)}) copy-start(bf16[1,128,2560]{1,2,0:T(8,128)(2,1)S(1)} %copy.103) | copy-start | bytes 1966084
  36.0 17.8 %collective-permute-start.3 = (bf16[128,1024]{0,1:T(8,128)(2,1)S(1)}, bf16[128,1024]{0,1:T(8,128)(2,1)S(1)}, u32[]{:S(2)}, u32[]{:S(2)}) collective-permute-start(bf16[128,1024]{0,1:T(8,128)(2,1)S(1)} %pad_maximum_fusion.1), channel_id=1, source_target_pairs={{0,5},{1,6},{2,7},{3,8},{4,9},{5,10},{6,11},{7,12},{8,13},{9,14},{... | collective-permute-start | bytes 786440 | tf_op jit(solution)/shard_map/ppermute | solution.py:19
  48.6 17.3 %collective-permute-start.4 = (bf16[128,1024]{0,1:T(8,128)(2,1)S(1)}, bf16[128,1024]{0,1:T(8,128)(2,1)S(1)}, u32[]{:S(2)}, u32[]{:S(2)}) collective-permute-start(bf16[128,1024]{0,1:T(8,128)(2,1)S(1)} %pad_maximum_fusion.1), channel_id=1, source_target_pairs={{0,4},{1,5},{2,6},{3,7},{4,8},{5,9},{6,10},{7,11},{8,12},{9,13},{1... | collective-permute-start | bytes 786440 | tf_op jit(solution)/shard_map/ppermute | solution.py:19
  50.6 16.7 %collective-permute-start.5 = (bf16[128,1024]{0,1:T(8,128)(2,1)S(1)}, bf16[128,1024]{0,1:T(8,128)(2,1)S(1)}, u32[]{:S(2)}, u32[]{:S(2)}) collective-permute-start(bf16[128,1024]{0,1:T(8,128)(2,1)S(1)} %pad_maximum_fusion.1), channel_id=1, source_target_pairs={{0,3},{1,4},{2,5},{3,6},{4,7},{5,8},{6,9},{7,10},{8,11},{9,12},{10... | collective-permute-start | bytes 786440 | tf_op jit(solution)/shard_map/ppermute | solution.py:19
  68.9 6.9 %copy-start.4 = (bf16[1152,512]{0,1:T(8,128)(2,1)}, bf16[1152,512]{0,1:T(8,128)(2,1)S(1)}, u32[]{:S(2)}) copy-start(bf16[1152,512]{0,1:T(8,128)(2,1)S(1)} %get-tuple-element.38) | copy-start | bytes 3538948
  92.2 5.6 %copy-start.8 = (bf16[1,128,2560]{1,2,0:T(8,128)(2,1)S(1)}, bf16[1,128,2560]{1,2,0:T(8,128)(2,1)}, u32[]{:S(2)}) copy-start(bf16[1,128,2560]{1,2,0:T(8,128)(2,1)} %copy-done.7) | copy-start | bytes 1966084
  104.2 130.4 %copy-start.2 = (f32[1152,512]{1,0:T(8,128)S(1)}, f32[1152,512]{1,0:T(8,128)}, u32[]{:S(2)}) copy-start(f32[1152,512]{1,0:T(8,128)} %copy.113) | copy-start | bytes 7077892
  106.2 52.8 %collective-permute-start.8 = (f32[128,1024]{1,0:T(8,128)S(1)}, f32[128,1024]{1,0:T(8,128)S(1)}, u32[]{:S(2)}, u32[]{:S(2)}) collective-permute-start(f32[128,1024]{1,0:T(8,128)S(1)} %get-tuple-element.30), channel_id=1, source_target_pairs={{1,0},{2,1},{3,2},{4,3},{5,4},{6,5},{7,6},{8,7},{9,8},{10,9},{11,1... | collective-permute-start | bytes 1572872 | tf_op jit(solution)/shard_map/ppermute | solution.py:19
  110.6 50.4 %collective-permute-start.9 = (f32[128,1024]{1,0:T(8,128)S(1)}, f32[128,1024]{1,0:T(8,128)S(1)}, u32[]{:S(2)}, u32[]{:S(2)}) collective-permute-start(f32[128,1024]{1,0:T(8,128)S(1)} %get-tuple-element.31), channel_id=1, source_target_pairs={{2,0},{3,1},{4,2},{5,3},{6,4},{7,5},{8,6},{9,7},{10,8},{11,9},{12,... | collective-permute-start | bytes 1572872 | tf_op jit(solution)/shard_map/ppermute | solution.py:19
  112.5 53.7 %collective-permute-start.10 = (f32[128,1024]{1,0:T(8,128)S(1)}, f32[128,1024]{1,0:T(8,128)S(1)}, u32[]{:S(2)}, u32[]{:S(2)}) collective-permute-start(f32[128,1024]{1,0:T(8,128)S(1)} %get-tuple-element.32), channel_id=1, source_target_pairs={{3,0},{4,1},{5,2},{6,3},{7,4},{8,5},{9,6},{10,7},{11,8},{12,9},{13... | collective-permute-start | bytes 1572872 | tf_op jit(solution)/shard_map/ppermute | solution.py:19
  114.6 72.4 %collective-permute-start.11 = (f32[128,1024]{1,0:T(8,128)S(1)}, f32[128,1024]{1,0:T(8,128)S(1)}, u32[]{:S(2)}, u32[]{:S(2)}) collective-permute-start(f32[128,1024]{1,0:T(8,128)S(1)} %get-tuple-element.33), channel_id=1, source_target_pairs={{4,0},{5,1},{6,2},{7,3},{8,4},{9,5},{10,6},{11,7},{12,8},{13,9},{1... | collective-permute-start | bytes 1572872 | tf_op jit(solution)/shard_map/ppermute | solution.py:19
  116.5 86.1 %collective-permute-start.12 = (f32[128,1024]{1,0:T(8,128)S(1)}, f32[128,1024]{1,0:T(8,128)S(1)}, u32[]{:S(2)}, u32[]{:S(2)}) collective-permute-start(f32[128,1024]{1,0:T(8,128)S(1)} %get-tuple-element.34), channel_id=1, source_target_pairs={{5,0},{6,1},{7,2},{8,3},{9,4},{10,5},{11,6},{12,7},{13,8},{14,9},{... | collective-permute-start | bytes 1572872 | tf_op jit(solution)/shard_map/ppermute | solution.py:19
  159.0 54.8 %collective-permute-start.13 = (f32[128,1024]{1,0:T(8,128)S(1)}, f32[128,1024]{1,0:T(8,128)S(1)}, u32[]{:S(2)}, u32[]{:S(2)}) collective-permute-start(f32[128,1024]{1,0:T(8,128)S(1)} %get-tuple-element.35), channel_id=1, source_target_pairs={{6,0},{7,1},{8,2},{9,3},{10,4},{11,5},{12,6},{13,7},{14,8},{15,9},... | collective-permute-start | bytes 1572872 | tf_op jit(solution)/shard_map/ppermute | solution.py:19
  160.9 66.6 %collective-permute-start.15 = (f32[128,1024]{1,0:T(8,128)S(1)}, f32[128,1024]{1,0:T(8,128)S(1)}, u32[]{:S(2)}, u32[]{:S(2)}) collective-permute-start(f32[128,1024]{1,0:T(8,128)S(1)} %get-tuple-element.36), channel_id=1, source_target_pairs={{8,0},{9,1},{10,2},{11,3},{12,4},{13,5},{14,6},{15,7},{16,8},{17,9... | collective-permute-start | bytes 1572872 | tf_op jit(solution)/shard_map/ppermute | solution.py:19
  166.2 68.4 %collective-permute-start.14 = (f32[128,1024]{1,0:T(8,128)S(1)}, f32[128,1024]{1,0:T(8,128)S(1)}, u32[]{:S(2)}, u32[]{:S(2)}) collective-permute-start(f32[128,1024]{1,0:T(8,128)S(1)} %get-tuple-element.37), channel_id=1, source_target_pairs={{7,0},{8,1},{9,2},{10,3},{11,4},{12,5},{13,6},{14,7},{15,8},{16,9}... | collective-permute-start | bytes 1572872 | tf_op jit(solution)/shard_map/ppermute | solution.py:19
  235.7 115.2 %reduce-scatter.4.cloned.1.call-start = ((), (), s32[]{:S(2)}) async-start(), calls=%async_computation.2 | async-start | bytes 2949120 | tf_op jit(solution)/shard_map/reduce_scatter | solution.py:121
  243.5 15.0 %collective-permute-start.16 = (bf16[128,640]{1,0:T(8,128)(2,1)}, bf16[128,640]{1,0:T(8,128)(2,1)S(1)}, u32[]{:S(2)}, u32[]{:S(2)}) collective-permute-start(bf16[128,640]{1,0:T(8,128)(2,1)} %bitcast.36), channel_id=1, source_target_pairs={{0,7},{1,0},{2,1},{3,2},{4,3},{5,4},{6,5},{7,6},{8,15},{9,8},{10,9... | collective-permute-start | bytes 491528 | tf_op jit(solution)/shard_map/ppermute | solution.py:46
  245.3 15.1 %collective-permute-start.17 = (bf16[128,640]{1,0:T(8,128)(2,1)}, bf16[128,640]{1,0:T(8,128)(2,1)S(1)}, u32[]{:S(2)}, u32[]{:S(2)}) collective-permute-start(bf16[128,640]{1,0:T(8,128)(2,1)} %bitcast.37), channel_id=1, source_target_pairs={{0,6},{1,7},{2,0},{3,1},{4,2},{5,3},{6,4},{7,5},{8,14},{9,15},{10,... | collective-permute-start | bytes 491528 | tf_op jit(solution)/shard_map/ppermute | solution.py:46
  245.5 18.1 %collective-permute-start.18 = (bf16[128,640]{1,0:T(8,128)(2,1)S(1)}, bf16[128,640]{1,0:T(8,128)(2,1)S(1)}, u32[]{:S(2)}, u32[]{:S(2)}) collective-permute-start(bf16[128,640]{1,0:T(8,128)(2,1)S(1)} %bitcast.115), channel_id=1, source_target_pairs={{0,5},{1,6},{2,7},{3,0},{4,1},{5,2},{6,3},{7,4},{8,13},{9,14},{10,... | collective-permute-start | bytes 491528 | tf_op jit(solution)/shard_map/ppermute | solution.py:46
  245.8 18.5 %collective-permute-start.19 = (bf16[128,640]{1,0:T(8,128)(2,1)S(1)}, bf16[128,640]{1,0:T(8,128)(2,1)S(1)}, u32[]{:S(2)}, u32[]{:S(2)}) collective-permute-start(bf16[128,640]{1,0:T(8,128)(2,1)S(1)} %bitcast.113), channel_id=1, source_target_pairs={{0,4},{1,5},{2,6},{3,7},{4,0},{5,1},{6,2},{7,3},{8,12},{9,13},{10,... | collective-permute-start | bytes 491528 | tf_op jit(solution)/shard_map/ppermute | solution.py:46
  253.5 16.6 %collective-permute-start.20 = (bf16[128,640]{1,0:T(8,128)(2,1)S(1)}, bf16[128,640]{1,0:T(8,128)(2,1)S(1)}, u32[]{:S(2)}, u32[]{:S(2)}) collective-permute-start(bf16[128,640]{1,0:T(8,128)(2,1)S(1)} %bitcast.112), channel_id=1, source_target_pairs={{0,3},{1,4},{2,5},{3,6},{4,7},{5,0},{6,1},{7,2},{8,11},{9,12},{10,... | collective-permute-start | bytes 491528 | tf_op jit(solution)/shard_map/ppermute | solution.py:46
  258.5 12.2 %collective-permute-start.21 = (bf16[128,640]{1,0:T(8,128)(2,1)S(1)}, bf16[128,640]{1,0:T(8,128)(2,1)S(1)}, u32[]{:S(2)}, u32[]{:S(2)}) collective-permute-start(bf16[128,640]{1,0:T(8,128)(2,1)S(1)} %bitcast.116), channel_id=1, source_target_pairs={{0,2},{1,3},{2,4},{3,5},{4,6},{5,7},{6,0},{7,1},{8,10},{9,11},{10,... | collective-permute-start | bytes 491528 | tf_op jit(solution)/shard_map/ppermute | solution.py:46
  260.4 15.6 %collective-permute-start.22 = (bf16[128,640]{1,0:T(8,128)(2,1)S(1)}, bf16[128,640]{1,0:T(8,128)(2,1)S(1)}, u32[]{:S(2)}, u32[]{:S(2)}) collective-permute-start(bf16[128,640]{1,0:T(8,128)(2,1)S(1)} %bitcast.114), channel_id=1, source_target_pairs={{0,1},{1,2},{2,3},{3,4},{4,5},{5,6},{6,7},{7,0},{8,9},{9,10},{10,1... | collective-permute-start | bytes 491528 | tf_op jit(solution)/shard_map/ppermute | solution.py:46
  312.7 51.9 %copy-start.9 = (bf16[128,1024]{1,0:T(8,128)(2,1)S(1)}, bf16[128,1024]{1,0:T(8,128)(2,1)}, u32[]{:S(2)}) copy-start(bf16[128,1024]{1,0:T(8,128)(2,1)} %fusion.36) | copy-start | bytes 786436
  362.7 7.1 %collective-permute-start.23 = (f32[12,1024]{1,0:T(8,128)S(1)}, f32[12,1024]{1,0:T(8,128)S(1)}, u32[]{:S(2)}, u32[]{:S(2)}) collective-permute-start(f32[12,1024]{1,0:T(8,128)S(1)} %slice.72), channel_id=1, source_target_pairs={{0,64},{64,128},{128,192},{1,65},{65,129},{129,193},{2,66},{66,130... | collective-permute-start | bytes 147464
  (7 other events, 20.7 us)
Sparse Core Ops, SparseCore 0:
  235.8 65.8 all-gather.1
  307.0 43.8 reduce-scatter.3
